TPU v7x, 32 devices: a whole 2x2x4 slice. The times are simulated.
32 devices in a mesh: pipe: 2 (over x), dp: 4 (over z), mp: 4 (over y, core).
Axes of the slice: x: 2, y: 2, z: 4, core: 2. Of those that a mesh axis runs over, the one named last changes fastest.
Arguments:
- section_in: bfloat16 [2, 12, 729, 1152], P('pipe', 'dp'), may hold values from -6 to 6
- ln1_gain: bfloat16 [2, 1152], P('pipe'), may hold values from 0.099609375 to 1.8984375
- ln1_bias: bfloat16 [2, 1152], P('pipe'), may hold values from -3 to 3
- qkv_weight: bfloat16 [2, 1152, 3, 1152], P('pipe', None, None, 'mp'), may hold values from -0.1875 to 0.1875
- qv_bias: bfloat16 [2, 2, 1152], P('pipe', None, 'mp'), may hold values from -3 to 3
- out_weight: bfloat16 [2, 1152, 1152], P('pipe', 'mp'), may hold values from -3 to 3
- out_bias: bfloat16 [2, 1152], P('pipe'), may hold values from -3 to 3
- ln2_gain: bfloat16 [2, 1152], P('pipe'), may hold values from 0.099609375 to 1.8984375
- ln2_bias: bfloat16 [2, 1152], P('pipe'), may hold values from -3 to 3
- fc1_weight: bfloat16 [2, 1152, 4304], P('pipe', None, 'mp'), may hold values from -0.1875 to 0.1875
- fc1_bias: bfloat16 [2, 4304], P('pipe', 'mp'), may hold values from -3 to 3
- fc2_weight: bfloat16 [2, 4304, 1152], P('pipe', 'mp'), may hold values from -0.1875 to 0.1875
- fc2_bias: bfloat16 [2, 1152], P('pipe'), may hold values from -4 to 4
Outputs:
- section_out: bfloat16 [2, 12, 729, 1152], P('pipe', 'dp')
- grad_ln1_gain: float32 [2, 1152], P('pipe')
- grad_ln1_bias: float32 [2, 1152], P('pipe')
- grad_qkv_weight: float32 [2, 1152, 3, 1152], P('pipe', None, None, 'mp')
- grad_qv_bias: float32 [2, 2, 1152], P('pipe', None, 'mp')
- grad_out_weight: float32 [2, 1152, 1152], P('pipe', 'mp')
- grad_out_bias: float32 [2, 1152], P('pipe')
- grad_ln2_gain: float32 [2, 1152], P('pipe')
- grad_ln2_bias: float32 [2, 1152], P('pipe')
- grad_fc1_weight: float32 [2, 1152, 4304], P('pipe', None, 'mp')
- grad_fc1_bias: float32 [2, 4304], P('pipe', 'mp')
- grad_fc2_weight: float32 [2, 4304, 1152], P('pipe', 'mp')
- grad_fc2_bias: float32 [2, 1152], P('pipe')
All inputs are finite; a program needn't handle non-finite values.
Results may differ from a plain program's by a relative error of at most 0.028.
Values may be sent and summed in bfloat16 or wider, within the bound.
A program may use at most 320 MiB of HBM per device.

v0:
```python
import jax
import jax.numpy as jnp
from jax import lax
from jax.sharding import PartitionSpec as P

HDIM = 72
EPSILON = 1e-06
GELU_SCALE = 0.7978845608028654
GELU_CUBIC = 0.044715


def shifted(value, axis, by):
    peers = lax.axis_size(axis)
    pairs = [(i, i + by) for i in range(peers) if 0 <= i + by < peers]
    return lax.ppermute(value, axis, pairs)


def norm_rows(values, gain_vec, shift_vec):
    center = values - jnp.mean(values, axis=-1, keepdims=True)
    inv_std = lax.rsqrt(jnp.mean(center * center, axis=-1, keepdims=True) + EPSILON)
    x_hat = center * inv_std
    return (x_hat * gain_vec + shift_vec, x_hat, inv_std)


def norm_back(d_out, x_hat, inv_std, gain_vec):
    d_hat = d_out * gain_vec
    inner = (
        d_hat
        - jnp.mean(d_hat, axis=-1, keepdims=True)
        - x_hat * jnp.mean(d_hat * x_hat, axis=-1, keepdims=True)
    )
    return (inv_std * inner, jnp.sum(d_out * x_hat, axis=0), jnp.sum(d_out, axis=0))


def gelu_parts(pre_act):
    tanh_val = jnp.tanh(GELU_SCALE * (pre_act + GELU_CUBIC * pre_act * pre_act * pre_act))
    act_value = 0.5 * pre_act * (1.0 + tanh_val)
    act_slope = 0.5 * (1.0 + tanh_val) + 0.5 * pre_act * (
        1.0 - tanh_val * tanh_val
    ) * GELU_SCALE * (1.0 + 3.0 * GELU_CUBIC * pre_act * pre_act)
    return (act_value, act_slope)


def attend(query, key_rows, value_rows, scaling):
    scores = (
        jnp.einsum("qhd,khd->hqk", query, key_rows, preferred_element_type=jnp.float32) * scaling
    )
    row_max = jnp.max(scores, axis=-1, keepdims=True)
    exp_terms = jnp.exp(scores - row_max)
    row_total = jnp.sum(exp_terms, axis=-1, keepdims=True)
    attn_probs = (exp_terms / row_total).astype(jnp.bfloat16)
    mixed = jnp.einsum("hqk,khd->qhd", attn_probs, value_rows, preferred_element_type=jnp.float32)
    return (mixed, row_max + jnp.log(row_total))


def attend_back(query, key_rows, value_rows, log_total, d_mixed, scaling):
    scores = (
        jnp.einsum("qhd,khd->hqk", query, key_rows, preferred_element_type=jnp.float32) * scaling
    )
    attn_probs = jnp.exp(scores - log_total)
    probs_low = attn_probs.astype(jnp.bfloat16)
    d_values = jnp.einsum("hqk,qhd->khd", probs_low, d_mixed, preferred_element_type=jnp.float32)
    d_probs = jnp.einsum("qhd,khd->hqk", d_mixed, value_rows, preferred_element_type=jnp.float32)
    inner = jnp.sum(d_probs * attn_probs, axis=-1, keepdims=True)
    d_scores = (attn_probs * (d_probs - inner)).astype(jnp.bfloat16)
    d_query = (
        jnp.einsum("hqk,khd->qhd", d_scores, key_rows, preferred_element_type=jnp.float32) * scaling
    )
    d_keys = (
        jnp.einsum("hqk,qhd->khd", d_scores, query, preferred_element_type=jnp.float32) * scaling
    )
    return (
        d_query.astype(jnp.bfloat16),
        d_keys.astype(jnp.bfloat16),
        d_values.astype(jnp.bfloat16),
    )


def attention_part(residual, gain_one, shift_one, w_qkv, bias_qv, scaling):
    row_count = residual.shape[0]
    normed = norm_rows(residual, gain_one, shift_one)[0]
    packed = jnp.dot(
        normed.astype(jnp.bfloat16), w_qkv, preferred_element_type=jnp.float32
    ).reshape(row_count, 3, -1)
    bias_three = jnp.stack([bias_qv[0], jnp.zeros_like(bias_qv[0]), bias_qv[1]])
    packed = (packed + bias_three).astype(jnp.bfloat16)
    local_width = packed.shape[2]
    head_count = local_width // HDIM
    query = packed[:, 0].reshape(row_count, head_count, HDIM)
    key_rows = packed[:, 1].reshape(row_count, head_count, HDIM)
    value_rows = packed[:, 2].reshape(row_count, head_count, HDIM)
    mixed, log_total = attend(query, key_rows, value_rows, scaling)
    return (packed, log_total, mixed.reshape(row_count, local_width).astype(jnp.bfloat16))


def attention_back(packed, log_total, d_attn, mixed_low, w_out, scaling):
    row_count = packed.shape[0]
    local_width = packed.shape[2]
    head_count = local_width // HDIM
    grad_w_out = jnp.einsum("sc,sd->cd", mixed_low, d_attn, preferred_element_type=jnp.float32)
    d_mixed = jnp.einsum("sd,cd->sc", d_attn, w_out, preferred_element_type=jnp.float32).astype(
        jnp.bfloat16
    )
    query = packed[:, 0].reshape(row_count, head_count, HDIM)
    key_rows = packed[:, 1].reshape(row_count, head_count, HDIM)
    value_rows = packed[:, 2].reshape(row_count, head_count, HDIM)
    d_query, d_keys, d_values = attend_back(
        query,
        key_rows,
        value_rows,
        log_total,
        d_mixed.reshape(row_count, head_count, HDIM),
        scaling,
    )
    d_query = d_query.reshape(row_count, local_width)
    d_values = d_values.reshape(row_count, local_width)
    d_packed = jnp.stack(
        [d_query, d_keys.reshape(row_count, local_width), d_values], axis=1
    ).reshape(row_count, 3 * local_width)
    grad_bias_qv = jnp.stack(
        [
            jnp.sum(d_query.astype(jnp.float32), axis=0),
            jnp.sum(d_values.astype(jnp.float32), axis=0),
        ]
    )
    return (grad_w_out, d_packed, grad_bias_qv)


def layer_forward(inputs, weights, scaling):
    (
        gain_one,
        shift_one,
        w_qkv,
        bias_qv,
        w_out,
        bias_out,
        gain_two,
        shift_two,
        w_fc1,
        bias_fc1,
        w_fc2,
        bias_fc2,
    ) = weights
    residual = inputs.astype(jnp.float32)
    packed, log_total, mixed_low = attention_part(
        residual, gain_one, shift_one, w_qkv, bias_qv, scaling
    )
    branch = lax.psum(
        jnp.dot(mixed_low, w_out, preferred_element_type=jnp.float32).astype(jnp.bfloat16), "mp"
    ).astype(jnp.float32)
    mid_stream = residual + branch + bias_out
    normed_two = norm_rows(mid_stream, gain_two, shift_two)[0]
    pre_act = (
        jnp.dot(normed_two.astype(jnp.bfloat16), w_fc1, preferred_element_type=jnp.float32)
        + bias_fc1
    )
    act_out = gelu_parts(pre_act)[0]
    branch_two = lax.psum(
        jnp.dot(act_out.astype(jnp.bfloat16), w_fc2, preferred_element_type=jnp.float32).astype(
            jnp.bfloat16
        ),
        "mp",
    ).astype(jnp.float32)
    layer_out = (mid_stream + branch_two + bias_fc2).astype(jnp.bfloat16)
    kept_state = (inputs, packed, log_total, mixed_low, mid_stream)
    return (layer_out, kept_state)


def layer_backward(kept_state, d_out, weights, scaling):
    (
        gain_one,
        shift_one,
        w_qkv,
        bias_qv,
        w_out,
        bias_out,
        gain_two,
        shift_two,
        w_fc1,
        bias_fc1,
        w_fc2,
        bias_fc2,
    ) = weights
    inputs, packed, log_total, mixed_low, mid_stream = (
        kept_state[0],
        kept_state[1],
        kept_state[2],
        kept_state[3],
        kept_state[4],
    )
    residual = inputs.astype(jnp.float32)
    normed, hat_one, std_one = norm_rows(residual, gain_one, shift_one)
    normed_two, hat_two, std_two = norm_rows(mid_stream, gain_two, shift_two)
    normed_two_low = normed_two.astype(jnp.bfloat16)
    pre_act = jnp.dot(normed_two_low, w_fc1, preferred_element_type=jnp.float32) + bias_fc1
    act_out, act_slope = gelu_parts(pre_act)
    act_low = act_out.astype(jnp.bfloat16)
    grad_b_two = jnp.sum(d_out, axis=0)
    d_mlp = d_out.astype(jnp.bfloat16)
    grad_w_two = jnp.einsum("sf,sd->fd", act_low, d_mlp, preferred_element_type=jnp.float32)
    d_act = jnp.einsum("sd,fd->sf", d_mlp, w_fc2, preferred_element_type=jnp.float32)
    d_pre = (d_act * act_slope).astype(jnp.bfloat16)
    grad_w_one = jnp.einsum("sd,sf->df", normed_two_low, d_pre, preferred_element_type=jnp.float32)
    grad_b_one = jnp.sum(d_pre.astype(jnp.float32), axis=0)
    d_norm_two = lax.psum(
        jnp.einsum("sf,df->sd", d_pre, w_fc1, preferred_element_type=jnp.float32).astype(
            jnp.bfloat16
        ),
        "mp",
    ).astype(jnp.float32)
    d_mid_norm, grad_gain_two, grad_shift_two = norm_back(d_norm_two, hat_two, std_two, gain_two)
    d_mid = d_out + d_mid_norm
    grad_bias_out = jnp.sum(d_mid, axis=0)
    grad_w_out, d_packed, grad_bias_qv = attention_back(
        packed, log_total, d_mid.astype(jnp.bfloat16), mixed_low, w_out, scaling
    )
    grad_w_qkv = jnp.einsum(
        "sd,sc->dc", normed.astype(jnp.bfloat16), d_packed, preferred_element_type=jnp.float32
    )
    d_norm_one = lax.psum(
        jnp.einsum("sc,dc->sd", d_packed, w_qkv, preferred_element_type=jnp.float32).astype(
            jnp.bfloat16
        ),
        "mp",
    ).astype(jnp.float32)
    d_res_norm, grad_gain_one, grad_shift_one = norm_back(d_norm_one, hat_one, std_one, gain_one)
    d_input = (d_mid + d_res_norm).astype(jnp.bfloat16)
    grads = (
        grad_gain_one,
        grad_shift_one,
        grad_w_qkv,
        grad_bias_qv,
        grad_w_out,
        grad_bias_out,
        grad_gain_two,
        grad_shift_two,
        grad_w_one,
        grad_b_one,
        grad_w_two,
        grad_b_two,
    )
    return (d_input, grads)


def on_device(
    section_in,
    ln1_gain,
    ln1_bias,
    qkv_weight,
    qv_bias,
    out_weight,
    out_bias,
    ln2_gain,
    ln2_bias,
    fc1_weight,
    fc1_bias,
    fc2_weight,
    fc2_bias,
):
    section_pos = lax.axis_index("pipe")
    is_first = section_pos == 0
    feed_rows = section_in[0]
    micro_count = feed_rows.shape[0]
    model_width = feed_rows.shape[2]
    scaling = HDIM ** (-0.5)
    weights = (
        ln1_gain[0].astype(jnp.float32),
        ln1_bias[0].astype(jnp.float32),
        qkv_weight[0].reshape(model_width, -1),
        qv_bias[0].astype(jnp.float32),
        out_weight[0],
        out_bias[0].astype(jnp.float32),
        ln2_gain[0].astype(jnp.float32),
        ln2_bias[0].astype(jnp.float32),
        fc1_weight[0],
        fc1_bias[0].astype(jnp.float32),
        fc2_weight[0],
        fc2_bias[0].astype(jnp.float32),
    )

    def pick_side(low_side, high_side):
        return jnp.where(is_first, low_side, high_side)

    arriving = jnp.zeros(feed_rows.shape[1:], jnp.bfloat16)
    kept_ticks = []
    results = []
    for tick_num in range(micro_count + 1):
        pick_index = jnp.clip(tick_num - section_pos, 0, micro_count - 1)
        own_rows = lax.dynamic_index_in_dim(feed_rows, pick_index, 0, keepdims=False)
        layer_out, kept_state = layer_forward(
            jnp.where(is_first, own_rows, arriving), weights, scaling
        )
        kept_ticks.append(kept_state)
        results.append(layer_out)
        if tick_num < micro_count:
            arriving = shifted(layer_out, "pipe", 1)
    back_rows = jnp.zeros(feed_rows.shape[1:], jnp.bfloat16)
    totals = None
    sent_grads = []
    for tick_num in range(micro_count + 1):
        pick_index = jnp.clip(tick_num - 1 + section_pos, 0, micro_count - 1)
        own_rows = lax.dynamic_index_in_dim(feed_rows, pick_index, 0, keepdims=False)
        d_out = jnp.where(is_first, back_rows, own_rows).astype(jnp.float32)
        kept_state = jax.tree.map(
            pick_side, kept_ticks[max(tick_num - 1, 0)], kept_ticks[min(tick_num + 1, micro_count)]
        )
        d_input, grads = layer_backward(kept_state, d_out, weights, scaling)
        is_live = jnp.where(is_first, tick_num >= 1, tick_num < micro_count)
        grads = tuple((jnp.where(is_live, grad_item, 0.0) for grad_item in grads))
        totals = (
            grads
            if totals is None
            else tuple((left_item + right_item for left_item, right_item in zip(totals, grads)))
        )
        sent_grads.append(d_input)
        if tick_num < micro_count:
            back_rows = shifted(d_input, "pipe", -1)
    share_list = (
        lax.psum_scatter(
            totals[2].astype(jnp.bfloat16), "dp", scatter_dimension=0, tiled=True
        ).astype(jnp.float32),
        lax.psum_scatter(
            totals[4].astype(jnp.bfloat16), "dp", scatter_dimension=1, tiled=True
        ).astype(jnp.float32),
        lax.psum_scatter(
            totals[8].astype(jnp.bfloat16), "dp", scatter_dimension=0, tiled=True
        ).astype(jnp.float32),
        lax.psum_scatter(
            totals[10].astype(jnp.bfloat16), "dp", scatter_dimension=1, tiled=True
        ).astype(jnp.float32),
    )
    whole = (
        lax.all_gather(share_list[0].astype(jnp.bfloat16), "dp", axis=0, tiled=True).astype(
            jnp.float32
        ),
        lax.all_gather(share_list[1].astype(jnp.bfloat16), "dp", axis=1, tiled=True).astype(
            jnp.float32
        ),
        lax.all_gather(share_list[2].astype(jnp.bfloat16), "dp", axis=0, tiled=True).astype(
            jnp.float32
        ),
        lax.all_gather(share_list[3].astype(jnp.bfloat16), "dp", axis=1, tiled=True).astype(
            jnp.float32
        ),
    )
    small = lax.psum(
        (totals[0], totals[1], totals[3], totals[5], totals[6], totals[7], totals[9], totals[11]),
        "dp",
    )
    forward_rows = jnp.stack(results[1:])
    backward_rows = jnp.stack(sent_grads[1:])
    section_out = jnp.where(is_first, backward_rows, forward_rows)[None]
    return (
        section_out,
        small[0][None],
        small[1][None],
        whole[0].reshape(model_width, 3, -1)[None],
        small[2][None],
        whole[1][None],
        small[3][None],
        small[4][None],
        small[5][None],
        whole[2][None],
        small[6][None],
        whole[3][None],
        small[7][None],
    )


def solution(mesh):
    placed = (
        P("pipe", "dp", None, None),
        P("pipe", None),
        P("pipe", None),
        P("pipe", None, None, "mp"),
        P("pipe", None, "mp"),
        P("pipe", "mp", None),
        P("pipe", None),
        P("pipe", None),
        P("pipe", None),
        P("pipe", None, "mp"),
        P("pipe", "mp"),
        P("pipe", "mp", None),
        P("pipe", None),
    )
    return jax.shard_map(
        on_device,
        mesh=mesh,
        in_specs=placed,
        out_specs=(
            P("pipe", "dp", None, None),
            P("pipe", None),
            P("pipe", None),
            P("pipe", None, None, "mp"),
            P("pipe", None, "mp"),
            P("pipe", "mp", None),
            P("pipe", None),
            P("pipe", None),
            P("pipe", None),
            P("pipe", None, "mp"),
            P("pipe", "mp"),
            P("pipe", "mp", None),
            P("pipe", None),
        ),
        check_vma=False,
    )
```

profile of v0, /device:TPU:0, one launch (start us, length us, event | category | flops | bytes accessed | tf_op | source)
XLA Modules:
  0.0 1629.2 jit_solution(3938570287198335092)
XLA Ops:
  27.6 47.4 %all-reduce.18.cloned.1.call-done = bf16[729,1152]{1,0:T(8,128)(2,1)} async-done(((bf16[729,1152]{1,0:T(8,128)(2,1)}), bf16[729,1152]{1,0:T(8,128)(2,1)}) %all-reduce.18.cloned.1.call-update) | async-done | bytes 1679632 | tf_op jit(solution)/shard_map/psum | solution.py:148
  80.3 13.7 convolution_convert_fusion.15
  94.1 45.0 %all-reduce.20.cloned.1.call-done = bf16[729,1152]{1,0:T(8,128)(2,1)} async-done(((bf16[729,1152]{1,0:T(8,128)(2,1)}), bf16[729,1152]{1,0:T(8,128)(2,1)}) %all-reduce.20.cloned.1.call-update) | async-done | bytes 1679632 | tf_op jit(solution)/shard_map/psum | solution.py:158
  148.7 34.8 %collective-permute-done = bf16[729,1152]{1,0:T(8,128)(2,1)} collective-permute-done((bf16[729,1152]{1,0:T(8,128)(2,1)}, bf16[729,1152]{1,0:T(8,128)(2,1)}, u32[]{:S(2)}, u32[]{:S(2)}) %collective-permute-start) | collective-permute-done | bytes 1679648 | tf_op jit(solution)/shard_map/ppermute | solution.py:15
  202.0 46.4 %all-reduce.22.cloned.1.call-done = bf16[729,1152]{1,0:T(8,128)(2,1)} async-done(((bf16[729,1152]{1,0:T(8,128)(2,1)}), bf16[729,1152]{1,0:T(8,128)(2,1)}) %all-reduce.22.cloned.1.call-update) | async-done | bytes 1679632 | tf_op jit(solution)/shard_map/psum | solution.py:148
  258.2 7.0 convert_reduce_fusion.23
  270.2 13.9 convolution_convert_fusion.12
  284.2 72.7 %all-reduce.38.cloned.1.call-done = (bf16[729,1152]{1,0:T(8,128)(2,1)}, bf16[729,1152]{1,0:T(8,128)(2,1)}) async-done(((bf16[729,1152]{1,0:T(8,128)(2,1)}, bf16[729,1152]{1,0:T(8,128)(2,1)}), (bf16[729,1152]{1,0:T(8,128)(2,1)}, bf16[729,1152]{1,0:T(8,128)(2,1)})) %all-reduce.38.cloned.1.call-update) | async-done | bytes 3359248 | tf_op jit(solution)/shard_map/psum | solution.py:205
  369.8 30.1 %collective-permute-done.2 = bf16[729,1152]{1,0:T(8,128)(2,1)S(1)} collective-permute-done((bf16[729,1152]{1,0:T(8,128)(2,1)S(1)}, bf16[729,1152]{1,0:T(8,128)(2,1)S(1)}, u32[]{:S(2)}, u32[]{:S(2)}) %collective-permute-start.2) | collective-permute-done | bytes 1679648 | tf_op jit(solution)/shard_map/ppermute | solution.py:15
  413.0 10.2 multiply_convert_fusion.3
  447.0 71.8 %all-reduce.36.cloned.1.call-done = (bf16[729,1152]{1,0:T(8,128)(2,1)}, bf16[729,1152]{1,0:T(8,128)(2,1)}) async-done(((bf16[729,1152]{1,0:T(8,128)(2,1)}, bf16[729,1152]{1,0:T(8,128)(2,1)}), (bf16[729,1152]{1,0:T(8,128)(2,1)}, bf16[729,1152]{1,0:T(8,128)(2,1)})) %all-reduce.36.cloned.1.call-update) | async-done | bytes 3359248 | tf_op jit(solution)/shard_map/psum | solution.py:220
  530.8 36.7 %collective-permute-done.1 = bf16[729,1152]{1,0:T(8,128)(2,1)} collective-permute-done((bf16[729,1152]{1,0:T(8,128)(2,1)}, bf16[729,1152]{1,0:T(8,128)(2,1)}, u32[]{:S(2)}, u32[]{:S(2)}) %collective-permute-start.1) | collective-permute-done | bytes 1679648 | tf_op jit(solution)/shard_map/ppermute | solution.py:15
  567.5 6.9 fusion.440
  576.6 13.7 convolution_convert_fusion.9
  595.0 6.1 convert_reduce_fusion.22
  606.2 71.9 %all-reduce.34.cloned.1.call-done = (bf16[729,1152]{1,0:T(8,128)(2,1)}, bf16[729,1152]{1,0:T(8,128)(2,1)}) async-done(((bf16[729,1152]{1,0:T(8,128)(2,1)}, bf16[729,1152]{1,0:T(8,128)(2,1)}), (bf16[729,1152]{1,0:T(8,128)(2,1)}, bf16[729,1152]{1,0:T(8,128)(2,1)})) %all-reduce.34.cloned.1.call-update) | async-done | bytes 3359248 | tf_op jit(solution)/shard_map/psum | solution.py:205
  691.5 29.9 %collective-permute-done.4 = bf16[729,1152]{1,0:T(8,128)(2,1)S(1)} collective-permute-done((bf16[729,1152]{1,0:T(8,128)(2,1)S(1)}, bf16[729,1152]{1,0:T(8,128)(2,1)S(1)}, u32[]{:S(2)}, u32[]{:S(2)}) %collective-permute-start.4) | collective-permute-done | bytes 1679648 | tf_op jit(solution)/shard_map/ppermute | solution.py:15
  747.6 10.2 multiply_convert_fusion.2
  763.4 6.7 broadcast_select_fusion.11
  788.2 62.6 %all-reduce.32.cloned.1.call-done = (bf16[729,1152]{1,0:T(8,128)(2,1)}, bf16[729,1152]{1,0:T(8,128)(2,1)}) async-done(((bf16[729,1152]{1,0:T(8,128)(2,1)}, bf16[729,1152]{1,0:T(8,128)(2,1)}), (bf16[729,1152]{1,0:T(8,128)(2,1)}, bf16[729,1152]{1,0:T(8,128)(2,1)})) %all-reduce.32.cloned.1.call-update) | async-done | bytes 3359248 | tf_op jit(solution)/shard_map/psum | solution.py:220
  866.2 32.5 %collective-permute-done.3 = bf16[729,1152]{1,0:T(8,128)(2,1)S(1)} collective-permute-done((bf16[729,1152]{1,0:T(8,128)(2,1)S(1)}, bf16[729,1152]{1,0:T(8,128)(2,1)S(1)}, u32[]{:S(2)}, u32[]{:S(2)}) %collective-permute-start.3) | collective-permute-done | bytes 1679648 | tf_op jit(solution)/shard_map/ppermute | solution.py:15
  901.4 5.6 convert_reduce_fusion.21
  912.4 6.2 fusion.453
  922.9 33.5 %all-reduce.24.cloned.1.call-done = bf16[729,1152]{1,0:T(8,128)(2,1)} async-done(((bf16[729,1152]{1,0:T(8,128)(2,1)}), bf16[729,1152]{1,0:T(8,128)(2,1)}) %all-reduce.24.cloned.1.call-update) | async-done | bytes 1679632 | tf_op jit(solution)/shard_map/psum | solution.py:205
  967.1 6.6 convert_reduce_fusion.26
  978.5 10.2 multiply_convert_fusion.1
  1000.7 42.8 %all-reduce.26.cloned.1.call-done = bf16[729,1152]{1,0:T(8,128)(2,1)} async-done(((bf16[729,1152]{1,0:T(8,128)(2,1)}), bf16[729,1152]{1,0:T(8,128)(2,1)}) %all-reduce.26.cloned.1.call-update) | async-done | bytes 1679632 | tf_op jit(solution)/shard_map/psum | solution.py:220
  1056.3 34.5 %collective-permute-done.5 = bf16[729,1152]{1,0:T(8,128)(2,1)S(1)} collective-permute-done((bf16[729,1152]{1,0:T(8,128)(2,1)S(1)}, bf16[729,1152]{1,0:T(8,128)(2,1)S(1)}, u32[]{:S(2)}, u32[]{:S(2)}) %collective-permute-start.5) | collective-permute-done | bytes 1679648 | tf_op jit(solution)/shard_map/ppermute | solution.py:15
  1105.4 6.2 fusion.235
  1111.6 35.5 %all-reduce.28.cloned.1.call-done = bf16[729,1152]{1,0:T(8,128)(2,1)} async-done(((bf16[729,1152]{1,0:T(8,128)(2,1)}), bf16[729,1152]{1,0:T(8,128)(2,1)}) %all-reduce.28.cloned.1.call-update) | async-done | bytes 1679632 | tf_op jit(solution)/shard_map/psum | solution.py:205
  1156.7 5.4 convert_reduce_fusion.24
  1167.0 10.2 multiply_convert_fusion
  1202.9 6.5 fusion.5
  1209.7 7.9 fusion.432
  1224.7 13.9 convolution_convert_fusion.4
  1238.6 7.9 fusion.433
  1250.7 8.8 fusion.1
  1265.0 24.7 %reduce-scatter.11.cloned.1.call-done = bf16[1076,288]{0,1:T(8,128)(2,1)} async-done(((bf16[1076,1152]{0,1:T(8,128)(2,1)}), bf16[1076,288]{0,1:T(8,128)(2,1)}) %reduce-scatter.11.cloned.1.call-update) | async-done | bytes 619792 | tf_op jit(solution)/shard_map/reduce_scatter | solution.py:328
  1290.8 25.6 %reduce-scatter.15.cloned.1.call-done = bf16[288,288]{1,0:T(8,128)(2,1)} async-done(((bf16[1152,288]{1,0:T(8,128)(2,1)}), bf16[288,288]{1,0:T(8,128)(2,1)}) %reduce-scatter.15.cloned.1.call-update) | async-done | bytes 165904
  1316.4 18.8 %all_gather.13 = bf16[288,1152]{0,1:T(8,128)(2,1)S(1)} all-gather(bf16[288,288]{0,1:T(8,128)(2,1)} %bitcast.466), channel_id=1, replica_groups=mesh['pipe'=2,'dp'=4,'mp'=4] {'dp'}, dimensions={1}, use_global_device_ids=true | all-gather | bytes 829440 | tf_op jit(solution)/shard_map/all_gather | solution.py:336
  1339.7 51.4 %all-reduce.30.cloned.1.call-done = (bf16[729,1152]{1,0:T(8,128)(2,1)}, bf16[729,1152]{1,0:T(8,128)(2,1)}) async-done(((bf16[729,1152]{1,0:T(8,128)(2,1)}, bf16[729,1152]{1,0:T(8,128)(2,1)}), (bf16[729,1152]{1,0:T(8,128)(2,1)}, bf16[729,1152]{1,0:T(8,128)(2,1)})) %all-reduce.30.cloned.1.call-update) | async-done | bytes 3359248 | tf_op jit(solution)/shard_map/psum | solution.py:220
  1394.7 22.3 %all-reduce = (f32[1,1152]{1,0:T(1,128)}, f32[1,1152]{1,0:T(1,128)}, f32[1,2,288]{2,1,0:T(2,128)}, f32[1,1152]{1,0:T(1,128)}, f32[1,1152]{1,0:T(1,128)}, /*index...) all-reduce(f32[1,1152]{1,0:T(1,128)S(1)} %broadcast_in_dim.101, ...), channel_id=1, replica_groups=mesh['pipe'=2,'dp'=4,'mp'=4] {'dp'}, use_global_device_ids=true, to_apply=%region_80.81 | all-reduce | flops 8564 | bytes 68512 | tf_op jit(solution)/shard_map/psum | solution.py:346
  1421.5 26.0 %reduce-scatter.9.cloned.1.call-done = bf16[288,1076]{1,0:T(8,128)(2,1)} async-done(((bf16[1152,1076]{1,0:T(8,128)(2,1)}), bf16[288,1076]{1,0:T(8,128)(2,1)}) %reduce-scatter.9.cloned.1.call-update) | async-done | bytes 619792 | tf_op jit(solution)/shard_map/reduce_scatter | solution.py:325
  1456.2 37.6 %all-gather.4.cloned.1.call-done = bf16[1152,864]{1,0:T(8,128)(2,1)} async-done(((bf16[288,864]{1,0:T(8,128)(2,1)}), bf16[1152,864]{1,0:T(8,128)(2,1)}) %all-gather.4.cloned.1.call-update) | async-done | bytes 1990672 | tf_op jit(solution)/shard_map/all_gather | solution.py:333
  1501.6 47.7 %all-gather.8.cloned.1.call-done = bf16[1076,1152]{0,1:T(8,128)(2,1)} async-done(((bf16[1076,288]{0,1:T(8,128)(2,1)}), bf16[1076,1152]{0,1:T(8,128)(2,1)}) %all-gather.8.cloned.1.call-update) | async-done | bytes 2479120 | tf_op jit(solution)/shard_map/all_gather | solution.py:342
  1553.8 12.8 copy.131
  1566.5 38.3 %all-gather.6.cloned.1.call-done = bf16[1152,1076]{1,0:T(8,128)(2,1)} async-done(((bf16[288,1076]{1,0:T(8,128)(2,1)}), bf16[1152,1076]{1,0:T(8,128)(2,1)}) %all-gather.6.cloned.1.call-update) | async-done | bytes 2479120 | tf_op jit(solution)/shard_map/all_gather | solution.py:339
  1609.3 12.7 copy.130
  (632 shorter events, 381.8 us)
Async XLA Ops:
  7.2 73.1 %copy-start = (bf16[1,1152,1076]{1,2,0:T(8,128)(2,1)S(1)}, bf16[1,1152,1076]{1,2,0:T(8,128)(2,1)}, u32[]{:S(2)}) copy-start(bf16[1,1152,1076]{1,2,0:T(8,128)(2,1)} %param.22) | copy-start | bytes 7437316
  7.2 67.8 %all-reduce.18.cloned.1.call-start = ((), (), s32[]{:S(2)}) async-start(), calls=%async_computation.4 | async-start | bytes 3391488 | tf_op jit(solution)/shard_map/psum | solution.py:148
  27.2 111.9 %all-reduce.20.cloned.1.call-start = ((), (), s32[]{:S(2)}) async-start(), calls=%async_computation.5 | async-start | bytes 3391488 | tf_op jit(solution)/shard_map/psum | solution.py:158
  94.0 154.4 %all-reduce.22.cloned.1.call-start = ((), (), s32[]{:S(2)}) async-start(), calls=%async_computation.6 | async-start | bytes 3391488 | tf_op jit(solution)/shard_map/psum | solution.py:148
  94.1 584.1 %copy-start.108 = (f32[1152]{0:T(1024)}, f32[1152]{0:T(1024)S(1)}, u32[]{:S(2)}) copy-start(f32[1152]{0:T(1024)S(1)} %convert_reduce_fusion.32) | copy-start | bytes 13828
  143.7 39.8 %collective-permute-start = (bf16[729,1152]{1,0:T(8,128)(2,1)}, bf16[729,1152]{1,0:T(8,128)(2,1)}, u32[]{:S(2)}, u32[]{:S(2)}) collective-permute-start(bf16[729,1152]{1,0:T(8,128)(2,1)} %add_convert_fusion.10), channel_id=1, source_target_pairs={{0,16},{1,17},{2,18},{3,19},{4,20},{5,21},{6,22},{7,23},{8,24},{9,... | collective-permute-start | bytes 5038856 | tf_op jit(solution)/shard_map/ppermute | solution.py:15
  201.7 155.2 %all-reduce.38.cloned.1.call-start = ((), (), s32[]{:S(2)}) async-start(), calls=%async_computation.21 | async-start | bytes 6782976 | tf_op jit(solution)/shard_map/psum | solution.py:205
  255.0 144.8 %copy-start.110 = (f32[729]{0:T(1024)}, f32[729]{0:T(1024)S(1)}, u32[]{:S(2)}) copy-start(f32[729]{0:T(1024)S(1)} %broadcast_multiply_fusion.28) | copy-start | bytes 8752
  255.5 144.3 %copy-start.116 = (f32[729]{0:T(1024)}, f32[729]{0:T(1024)S(1)}, u32[]{:S(2)}) copy-start(f32[729]{0:T(1024)S(1)} %add_rsqrt_fusion.12) | copy-start | bytes 8752
  284.2 234.6 %all-reduce.36.cloned.1.call-start = ((), (), s32[]{:S(2)}) async-start(), calls=%async_computation.20 | async-start | bytes 6782976 | tf_op jit(solution)/shard_map/psum | solution.py:220
  360.4 39.5 %collective-permute-start.2 = (bf16[729,1152]{1,0:T(8,128)(2,1)S(1)}, bf16[729,1152]{1,0:T(8,128)(2,1)S(1)}, u32[]{:S(2)}, u32[]{:S(2)}) collective-permute-start(bf16[729,1152]{1,0:T(8,128)(2,1)S(1)} %add_convert_fusion.7), channel_id=1, source_target_pairs={{0,16},{1,17},{2,18},{3,19},{4,20},{5,21},{6,22},{7,23},{8,24},{9,... | collective-permute-start | bytes 5038856 | tf_op jit(solution)/shard_map/ppermute | solution.py:15
  364.4 35.4 %slice-start = ((s8[5087232]{0:T(1024)(128)(4,1)}), s8[4194304]{0:T(1024)(128)(4,1)S(1)}, s32[]{:S(2)}) async-start(s8[5087232]{0:T(1024)(128)(4,1)} %bitcast.390), calls=%async_computation.22 | async-start | bytes 8388608
  364.5 35.4 %slice-start.1 = ((s8[5087232]{0:T(1024)(128)(4,1)}), s8[892928]{0:T(1024)(128)(4,1)S(1)}, s32[]{:S(2)}) async-start(s8[5087232]{0:T(1024)(128)(4,1)} %bitcast.390), calls=%async_computation.23 | async-start | bytes 1785856
  365.9 42.3 %copy-start.1 = (f32[4,729,729]{1,2,0:T(8,128)}, f32[4,729,729]{1,2,0:T(8,128)S(1)}, u32[]{:S(2)}) copy-start(f32[4,729,729]{1,2,0:T(8,128)S(1)} %fusion.450) | copy-start | bytes 25509172
  444.8 233.3 %all-reduce.34.cloned.1.call-start = ((), (), s32[]{:S(2)}) async-start(), calls=%async_computation.19 | async-start | bytes 6782976 | tf_op jit(solution)/shard_map/psum | solution.py:205
  444.9 81.9 %copy-start.114 = (f32[729]{0:T(1024)}, f32[729]{0:T(1024)S(1)}, u32[]{:S(2)}) copy-start(f32[729]{0:T(1024)S(1)} %broadcast_multiply_fusion.25) | copy-start | bytes 8752
  446.9 79.8 %copy-start.120 = (f32[729]{0:T(1024)}, f32[729]{0:T(1024)S(1)}, u32[]{:S(2)}) copy-start(f32[729]{0:T(1024)S(1)} %add_rsqrt_fusion.11) | copy-start | bytes 8752
  526.7 40.8 %collective-permute-start.1 = (bf16[729,1152]{1,0:T(8,128)(2,1)}, bf16[729,1152]{1,0:T(8,128)(2,1)}, u32[]{:S(2)}, u32[]{:S(2)}) collective-permute-start(bf16[729,1152]{1,0:T(8,128)(2,1)} %fusion.121), channel_id=1, source_target_pairs={{16,0},{17,1},{18,2},{19,3},{20,4},{21,5},{22,6},{23,7},{24,8},{25... | collective-permute-start | bytes 5038856 | tf_op jit(solution)/shard_map/ppermute | solution.py:15
  528.0 39.5 %copy-start.4 = (bf16[729,1152]{1,0:T(8,128)(2,1)S(1)}, bf16[729,1152]{1,0:T(8,128)(2,1)}, u32[]{:S(2)}) copy-start(bf16[729,1152]{1,0:T(8,128)(2,1)} %get-tuple-element.155) | copy-start | bytes 5038852
  528.1 39.5 %copy-start.39 = (bf16[729,1152]{1,0:T(8,128)(2,1)S(1)}, bf16[729,1152]{1,0:T(8,128)(2,1)}, u32[]{:S(2)}) copy-start(bf16[729,1152]{1,0:T(8,128)(2,1)} %all-reduce.18.cloned.1.call-done) | copy-start | bytes 5038852
  574.4 113.1 %copy-start.112 = (f32[729]{0:T(1024)}, f32[729]{0:T(1024)S(1)}, u32[]{:S(2)}) copy-start(f32[729]{0:T(1024)S(1)} %broadcast_multiply_fusion.20) | copy-start | bytes 8752
  576.6 110.9 %copy-start.118 = (f32[729]{0:T(1024)}, f32[729]{0:T(1024)S(1)}, u32[]{:S(2)}) copy-start(f32[729]{0:T(1024)S(1)} %add_rsqrt_fusion.8) | copy-start | bytes 8752
  606.2 244.7 %all-reduce.32.cloned.1.call-start = ((), (), s32[]{:S(2)}) async-start(), calls=%async_computation.18 | async-start | bytes 6782976 | tf_op jit(solution)/shard_map/psum | solution.py:220
  681.7 39.7 %collective-permute-start.4 = (bf16[729,1152]{1,0:T(8,128)(2,1)S(1)}, bf16[729,1152]{1,0:T(8,128)(2,1)S(1)}, u32[]{:S(2)}, u32[]{:S(2)}) collective-permute-start(bf16[729,1152]{1,0:T(8,128)(2,1)S(1)} %add_convert_fusion.4), channel_id=1, source_target_pairs={{0,16},{1,17},{2,18},{3,19},{4,20},{5,21},{6,22},{7,23},{8,24},{9,... | collective-permute-start | bytes 5038856 | tf_op jit(solution)/shard_map/ppermute | solution.py:15
  689.8 31.6 %copy-start.5 = (bf16[729,1152]{1,0:T(8,128)(2,1)S(1)}, bf16[729,1152]{1,0:T(8,128)(2,1)}, u32[]{:S(2)}) copy-start(bf16[729,1152]{1,0:T(8,128)(2,1)} %get-tuple-element.155) | copy-start | bytes 5038852
  777.0 179.5 %all-reduce.24.cloned.1.call-start = ((), (), s32[]{:S(2)}) async-start(), calls=%async_computation.7 | async-start | bytes 3391488 | tf_op jit(solution)/shard_map/psum | solution.py:205
  858.2 40.6 %collective-permute-start.3 = (bf16[729,1152]{1,0:T(8,128)(2,1)S(1)}, bf16[729,1152]{1,0:T(8,128)(2,1)S(1)}, u32[]{:S(2)}, u32[]{:S(2)}) collective-permute-start(bf16[729,1152]{1,0:T(8,128)(2,1)S(1)} %fusion.114), channel_id=1, source_target_pairs={{16,0},{17,1},{18,2},{19,3},{20,4},{21,5},{22,6},{23,7},{24,8},{25... | collective-permute-start | bytes 5038856 | tf_op jit(solution)/shard_map/ppermute | solution.py:15
  866.2 40.8 %copy-start.172 = (f32[729,1076]{0,1:T(8,128)}, f32[729,1076]{0,1:T(8,128)S(1)}, u32[]{:S(2)}) copy-start(f32[729,1076]{0,1:T(8,128)S(1)} %convolution_add_fusion.3) | copy-start | bytes 9412852
  866.2 35.1 %copy-start.153 = (bf16[1,1076,1152]{2,1,0:T(8,128)(2,1)S(1)}, bf16[1,1076,1152]{2,1,0:T(8,128)(2,1)}, u32[]{:S(2)}) copy-start(bf16[1,1076,1152]{2,1,0:T(8,128)(2,1)} %param.24) | copy-start | bytes 7437316
  912.1 131.3 %all-reduce.26.cloned.1.call-start = ((), (), s32[]{:S(2)}) async-start(), calls=%async_computation.8 | async-start | bytes 3391488 | tf_op jit(solution)/shard_map/psum | solution.py:220
  998.3 148.8 %all-reduce.28.cloned.1.call-start = ((), (), s32[]{:S(2)}) async-start(), calls=%async_computation.9 | async-start | bytes 3391488 | tf_op jit(solution)/shard_map/psum | solution.py:205
  1050.2 40.7 %collective-permute-start.5 = (bf16[729,1152]{1,0:T(8,128)(2,1)S(1)}, bf16[729,1152]{1,0:T(8,128)(2,1)S(1)}, u32[]{:S(2)}, u32[]{:S(2)}) collective-permute-start(bf16[729,1152]{1,0:T(8,128)(2,1)S(1)} %fusion.107), channel_id=1, source_target_pairs={{16,0},{17,1},{18,2},{19,3},{20,4},{21,5},{22,6},{23,7},{24,8},{25... | collective-permute-start | bytes 5038856 | tf_op jit(solution)/shard_map/ppermute | solution.py:15
  1056.3 41.6 %copy-start.175 = (f32[729,1076]{0,1:T(8,128)}, f32[729,1076]{0,1:T(8,128)S(1)}, u32[]{:S(2)}) copy-start(f32[729,1076]{0,1:T(8,128)S(1)} %convolution_add_fusion.2) | copy-start | bytes 9412852
  1056.3 36.6 %copy-start.154 = (bf16[1,1076,1152]{2,1,0:T(8,128)(2,1)S(1)}, bf16[1,1076,1152]{2,1,0:T(8,128)(2,1)}, u32[]{:S(2)}) copy-start(bf16[1,1076,1152]{2,1,0:T(8,128)(2,1)} %param.24) | copy-start | bytes 7437316
  1102.9 161.5 %reduce-scatter.13.cloned.1.call-start = ((), (), s32[]{:S(2)}) async-start(), calls=%async_computation.15 | async-start | bytes 2580480 | tf_op jit(solution)/shard_map/reduce_scatter | solution.py:319
  1191.7 98.0 %reduce-scatter.11.cloned.1.call-start = ((), (), s32[]{:S(2)}) async-start(), calls=%async_computation.13 | async-start | bytes 3317760 | tf_op jit(solution)/shard_map/reduce_scatter | solution.py:328
  1209.4 106.9 %reduce-scatter.15.cloned.1.call-start = ((), (), s32[]{:S(2)}) async-start(), calls=%async_computation.16 | async-start | bytes 1105920
  1224.7 166.3 %all-reduce.30.cloned.1.call-start = ((), (), s32[]{:S(2)}) async-start(), calls=%async_computation.17 | async-start | bytes 6782976 | tf_op jit(solution)/shard_map/psum | solution.py:220
  1250.0 197.4 %reduce-scatter.9.cloned.1.call-start = ((), (), s32[]{:S(2)}) async-start(), calls=%async_computation.11 | async-start | bytes 3317760 | tf_op jit(solution)/shard_map/reduce_scatter | solution.py:325
  1264.3 26.2 %copy-start.123 = (f32[1152]{0:T(1024)S(1)}, f32[1152]{0:T(1024)}, u32[]{:S(2)}) copy-start(f32[1152]{0:T(1024)} %get-tuple-element.165) | copy-start | bytes 13828
  1264.3 229.5 %all-gather.4.cloned.1.call-start = ((), (), s32[]{:S(2)}) async-start(), calls=%async_computation.10 | async-start | bytes 2580480 | tf_op jit(solution)/shard_map/all_gather | solution.py:333
  1264.9 284.4 %all-gather.8.cloned.1.call-start = ((), (), s32[]{:S(2)}) async-start(), calls=%async_computation.14 | async-start | bytes 3317760 | tf_op jit(solution)/shard_map/all_gather | solution.py:342
  1289.7 315.1 %all-gather.6.cloned.1.call-start = ((), (), s32[]{:S(2)}) async-start(), calls=%async_computation.12 | async-start | bytes 3317760 | tf_op jit(solution)/shard_map/all_gather | solution.py:339
  1336.5 58.1 %copy-start.130 = (f32[1152]{0:T(1024)S(1)}, f32[1152]{0:T(1024)}, u32[]{:S(2)}) copy-start(f32[1152]{0:T(1024)} %get-tuple-element.88) | copy-start | bytes 13828
  1336.5 58.1 %copy-start.131 = (f32[1152]{0:T(1024)S(1)}, f32[1152]{0:T(1024)}, u32[]{:S(2)}) copy-start(f32[1152]{0:T(1024)} %get-tuple-element.108) | copy-start | bytes 13828
  1336.5 58.1 %copy-start.134 = (f32[1152]{0:T(1024)S(1)}, f32[1152]{0:T(1024)}, u32[]{:S(2)}) copy-start(f32[1152]{0:T(1024)} %get-tuple-element.90) | copy-start | bytes 13828
  1336.5 58.1 %copy-start.135 = (f32[1152]{0:T(1024)S(1)}, f32[1152]{0:T(1024)}, u32[]{:S(2)}) copy-start(f32[1152]{0:T(1024)} %get-tuple-element.109) | copy-start | bytes 13828
  1336.5 80.5 %copy-start.109 = (f32[1152]{0:T(1024)S(1)}, f32[1152]{0:T(1024)}, u32[]{:S(2)}) copy-start(f32[1152]{0:T(1024)} %copy-done.108) | copy-start | bytes 13828
  (163 other events, 1082.5 us)
Sparse Core Ops, SparseCore 0:
  27.3 47.6 all-reduce.17
  94.1 44.9 all-reduce.19
  201.9 46.4 all-reduce.21
  284.3 72.6 all-reduce.37
  444.9 73.7 all-reduce.35
  606.3 71.8 all-reduce.33
  777.1 73.7 all-reduce.31
  912.2 44.1 all-reduce.23
  998.5 44.9 all-reduce.25
  1103.1 44.0 all-reduce.27
  1191.8 43.1 reduce-scatter.12
  1237.7 51.9 reduce-scatter.10
  1292.0 24.2 reduce-scatter.14
  1319.3 71.6 all-reduce.29
  1393.7 53.6 reduce-scatter.8
  1448.9 44.8 all-gather.3
  1495.2 54.0 all-gather.7
  1550.8 54.0 all-gather.5
where the time goes:
time: 1640 us; the launch traced here: 1630 us
  waiting for transfers between devices  980 us (60%)
  matrix products  304 us (19%)
  other arithmetic  195 us (12%)
  local copies, waits for them, and re-layouts  72 us (4%)
  blocking collectives  41.1 us (3%)
  starting transfers between devices  19.7 us (1%)
  between operations  17.4 us (1%)
    psum x4, waiting for transfers between devices, layer_backward(): lax.psum(jnp.einsum('sc,dc->sd', d_packed, w_qkv, preferred_element_type=...  229 us
    psum x4, waiting for transfers between devices, layer_backward(): lax.psum(jnp.einsum('sf,df->sd', d_pre, w_fc1, preferred_element_type=jnp...  214 us
    ppermute x6, waiting for transfers between devices, shifted(): return lax.ppermute(value, axis, pairs)  199 us
    psum x2, waiting for transfers between devices, layer_forward(): lax.psum(jnp.dot(mixed_low, w_out, preferred_element_type=jnp.float32).as...  93.8 us
    unnamed x378, local copies, waits for them, and re-layouts  62.6 us
    dot_general x4, matrix products, layer_forward(): jnp.dot(act_out.astype(jnp.bfloat16), w_fc2, preferred_element_type=jnp.f...  55.3 us
    all_gather x1, waiting for transfers between devices, on_device(): lax.all_gather(share_list[3].astype(jnp.bfloat16), 'dp', axis=1, tiled=True)  47.7 us
    psum x1, waiting for transfers between devices, layer_forward(): lax.psum(jnp.dot(act_out.astype(jnp.bfloat16), w_fc2, preferred_element_t...  45 us
  transfers between devices with their start and end apart: 24, of which 23 were waited for; matrix products, arithmetic and copies ran while one was open for 10% of the time, Pallas kernels for 0%

commit v1 on v0

--- a/solution.py
+++ b/solution.py
@@ -1,3 +1,4 @@
+import functools
 import jax
 import jax.numpy as jnp
 from jax import lax
@@ -7,6 +8,39 @@
 EPSILON = 1e-06
 GELU_SCALE = 0.7978845608028654
 GELU_CUBIC = 0.044715
+
+
+def treat_the_zone(array_in, across, axis_no):
+    base_arr, a_next, f_now = (
+        lax.axis_size(across),
+        lax.axis_index(across),
+        array_in.shape[axis_no],
+    )
+    trail = [s * base_arr if hop_no == axis_no else s for hop_no, s in enumerate(array_in.shape)]
+    newest = lax.dynamic_update_slice_in_dim(
+        jnp.zeros(trail, array_in.dtype), array_in, a_next * f_now, axis=axis_no
+    )
+    upper = right_arr = array_in
+    for p in range(1, base_arr // 2 + 1):
+        upper = lax.ppermute(
+            upper, across, perm=[(hop_no, (hop_no + 1) % base_arr) for hop_no in range(base_arr)]
+        )
+        newest = lax.dynamic_update_slice_in_dim(
+            newest, upper, (a_next - p) % base_arr * f_now, axis=axis_no
+        )
+        if 2 * p < base_arr:
+            right_arr = lax.ppermute(
+                right_arr,
+                axis_name=across,
+                perm=[(hop_no, (hop_no - 1) % base_arr) for hop_no in range(base_arr)],
+            )
+            newest = lax.dynamic_update_slice_in_dim(
+                newest, right_arr, (a_next + p) % base_arr * f_now, axis=axis_no
+            )
+    return newest
+
+
+measure_space = functools.partial(treat_the_zone, across="dp", axis_no=1)
 
 
 def shifted(value, axis, by):
@@ -339,9 +373,7 @@
         lax.all_gather(share_list[2].astype(jnp.bfloat16), "dp", axis=0, tiled=True).astype(
             jnp.float32
         ),
-        lax.all_gather(share_list[3].astype(jnp.bfloat16), "dp", axis=1, tiled=True).astype(
-            jnp.float32
-        ),
+        measure_space(share_list[3].astype(jnp.bfloat16)).astype(jnp.float32),
     )
     small = lax.psum(
         (totals[0], totals[1], totals[3], totals[5], totals[6], totals[7], totals[9], totals[11]),

time: 1640 us -> 2260 us (1.38)
  local copies, waits for them, and re-layouts: 72 us -> 708 us
  waiting for transfers between devices: 980 us -> 887 us
  blocking collectives: 41.1 us -> 73.5 us
  starting transfers between devices: 19.7 us -> 43.3 us
    dynamic_update_slice x0 -> x4, local copies, waits for them, and re-layouts: none -> 629 us  [the longest x2 379 us: treat_the_zone(): lax.dynamic_update_slice_in_dim(newest, upper, (a_next - p) % base_arr *...]
    all_gather x1 -> x0, waiting for transfers between devices: 47.7 us -> none  [on_device(): lax.all_gather(share_list[3].astype(jnp.bfloat16), 'dp', axis=1, tiled=True)]
    all_gather x1, waiting for transfers between devices: 38.3 us -> 0.01 us  [on_device(): lax.all_gather(share_list[2].astype(jnp.bfloat16), 'dp', axis=0, tiled=True)]
    all_gather x1, waiting for transfers between devices: 37.6 us -> 0.01 us  [on_device(): lax.all_gather(share_list[0].astype(jnp.bfloat16), 'dp', axis=0, tiled=True)]
    unnamed x19 -> x18, waiting for transfers between devices: 26.4 us -> 0.78 us
    ppermute x0 -> x3, starting transfers between devices: none -> 23.9 us  [the longest x2 20.5 us: treat_the_zone(): lax.ppermute(upper, across, perm=[(hop_no, (hop_no + 1) % base_arr) for h...]
    psum x4, waiting for transfers between devices: 229 us -> 252 us  [layer_backward(): lax.psum(jnp.einsum('sc,dc->sd', d_packed, w_qkv, preferred_element_type=...]
    reduce_scatter x1, waiting for transfers between devices: 24.7 us -> 48.1 us  [on_device(): lax.psum_scatter(totals[10].astype(jnp.bfloat16), 'dp', scatter_dimension...]
  transfers between devices with their start and end apart: 24 -> 26, of which waited for: 23 -> 20; matrix products, arithmetic and copies ran while one was open for 10% -> 37% of each run, Pallas kernels for 0% -> 0%
where the time goes in v1:
time: 2260 us; the launch traced here: 2240 us
  waiting for transfers between devices  887 us (39%)
  local copies, waits for them, and re-layouts  708 us (31%)
  matrix products  313 us (14%)
  other arithmetic  198 us (9%)
  blocking collectives  73.5 us (3%)
  starting transfers between devices  43.3 us (2%)
    dynamic_update_slice x2, local copies, waits for them, and re-layouts, treat_the_zone(): lax.dynamic_update_slice_in_dim(newest, upper, (a_next - p) % base_arr *...  379 us
    psum x4, waiting for transfers between devices, layer_backward(): lax.psum(jnp.einsum('sc,dc->sd', d_packed, w_qkv, preferred_element_type=...  252 us
    psum x4, waiting for transfers between devices, layer_backward(): lax.psum(jnp.einsum('sf,df->sd', d_pre, w_fc1, preferred_element_type=jnp...  214 us
    ppermute x6, waiting for transfers between devices, shifted(): return lax.ppermute(value, axis, pairs)  199 us
    dynamic_update_slice x1, local copies, waits for them, and re-layouts, treat_the_zone(): lax.dynamic_update_slice_in_dim(newest, right_arr, (a_next + p) % base_ar...  190 us
    psum x2, waiting for transfers between devices, layer_forward(): lax.psum(jnp.dot(mixed_low, w_out, preferred_element_type=jnp.float32).as...  93.7 us
    dynamic_update_slice x1, local copies, waits for them, and re-layouts, treat_the_zone(): lax.dynamic_update_slice_in_dim(jnp.zeros(trail, array_in.dtype), array_i...  60.4 us
    dot_general x4, matrix products, layer_forward(): jnp.dot(act_out.astype(jnp.bfloat16), w_fc2, preferred_element_type=jnp.f...  55.1 us
  transfers between devices with their start and end apart: 26, of which 20 were waited for; matrix products, arithmetic and copies ran while one was open for 37% of the time, Pallas kernels for 0%

profile of v1, /device:TPU:0, one launch (start us, length us, event | category | flops | bytes accessed | tf_op | source)
XLA Modules:
  0.0 2240.4 jit_solution(4801928994172790844)
XLA Ops:
  27.5 47.4 %all-reduce.18.cloned.1.call-done = bf16[729,1152]{1,0:T(8,128)(2,1)} async-done(((bf16[729,1152]{1,0:T(8,128)(2,1)}), bf16[729,1152]{1,0:T(8,128)(2,1)}) %all-reduce.18.cloned.1.call-update) | async-done | bytes 1679632 | tf_op jit(solution)/shard_map/psum | solution.py:182
  80.3 13.7 convolution_convert_fusion.15
  94.1 45.0 %all-reduce.20.cloned.1.call-done = bf16[729,1152]{1,0:T(8,128)(2,1)} async-done(((bf16[729,1152]{1,0:T(8,128)(2,1)}), bf16[729,1152]{1,0:T(8,128)(2,1)}) %all-reduce.20.cloned.1.call-update) | async-done | bytes 1679632 | tf_op jit(solution)/shard_map/psum | solution.py:192
  148.5 35.0 %collective-permute-done = bf16[729,1152]{1,0:T(8,128)(2,1)} collective-permute-done((bf16[729,1152]{1,0:T(8,128)(2,1)}, bf16[729,1152]{1,0:T(8,128)(2,1)}, u32[]{:S(2)}, u32[]{:S(2)}) %collective-permute-start) | collective-permute-done | bytes 1679648 | tf_op jit(solution)/shard_map/ppermute | solution.py:49
  202.2 46.2 %all-reduce.22.cloned.1.call-done = bf16[729,1152]{1,0:T(8,128)(2,1)} async-done(((bf16[729,1152]{1,0:T(8,128)(2,1)}), bf16[729,1152]{1,0:T(8,128)(2,1)}) %all-reduce.22.cloned.1.call-update) | async-done | bytes 1679632 | tf_op jit(solution)/shard_map/psum | solution.py:182
  258.2 7.0 convert_reduce_fusion.23
  270.2 13.9 convolution_convert_fusion.12
  284.2 72.7 %all-reduce.38.cloned.1.call-done = (bf16[729,1152]{1,0:T(8,128)(2,1)}, bf16[729,1152]{1,0:T(8,128)(2,1)}) async-done(((bf16[729,1152]{1,0:T(8,128)(2,1)}, bf16[729,1152]{1,0:T(8,128)(2,1)}), (bf16[729,1152]{1,0:T(8,128)(2,1)}, bf16[729,1152]{1,0:T(8,128)(2,1)})) %all-reduce.38.cloned.1.call-update) | async-done | bytes 3359248 | tf_op jit(solution)/shard_map/psum | solution.py:239
  369.6 30.2 %collective-permute-done.2 = bf16[729,1152]{1,0:T(8,128)(2,1)S(1)} collective-permute-done((bf16[729,1152]{1,0:T(8,128)(2,1)S(1)}, bf16[729,1152]{1,0:T(8,128)(2,1)S(1)}, u32[]{:S(2)}, u32[]{:S(2)}) %collective-permute-start.2) | collective-permute-done | bytes 1679648 | tf_op jit(solution)/shard_map/ppermute | solution.py:49
  413.1 10.2 multiply_convert_fusion.3
  447.3 71.8 %all-reduce.36.cloned.1.call-done = (bf16[729,1152]{1,0:T(8,128)(2,1)}, bf16[729,1152]{1,0:T(8,128)(2,1)}) async-done(((bf16[729,1152]{1,0:T(8,128)(2,1)}, bf16[729,1152]{1,0:T(8,128)(2,1)}), (bf16[729,1152]{1,0:T(8,128)(2,1)}, bf16[729,1152]{1,0:T(8,128)(2,1)})) %all-reduce.36.cloned.1.call-update) | async-done | bytes 3359248 | tf_op jit(solution)/shard_map/psum | solution.py:254
  531.1 36.7 %collective-permute-done.1 = bf16[729,1152]{1,0:T(8,128)(2,1)} collective-permute-done((bf16[729,1152]{1,0:T(8,128)(2,1)}, bf16[729,1152]{1,0:T(8,128)(2,1)}, u32[]{:S(2)}, u32[]{:S(2)}) %collective-permute-start.1) | collective-permute-done | bytes 1679648 | tf_op jit(solution)/shard_map/ppermute | solution.py:49
  567.8 6.8 fusion.440
  576.9 13.7 convolution_convert_fusion.9
  606.2 71.9 %all-reduce.34.cloned.1.call-done = (bf16[729,1152]{1,0:T(8,128)(2,1)}, bf16[729,1152]{1,0:T(8,128)(2,1)}) async-done(((bf16[729,1152]{1,0:T(8,128)(2,1)}, bf16[729,1152]{1,0:T(8,128)(2,1)}), (bf16[729,1152]{1,0:T(8,128)(2,1)}, bf16[729,1152]{1,0:T(8,128)(2,1)})) %all-reduce.34.cloned.1.call-update) | async-done | bytes 3359248 | tf_op jit(solution)/shard_map/psum | solution.py:239
  691.7 29.6 %collective-permute-done.4 = bf16[729,1152]{1,0:T(8,128)(2,1)S(1)} collective-permute-done((bf16[729,1152]{1,0:T(8,128)(2,1)S(1)}, bf16[729,1152]{1,0:T(8,128)(2,1)S(1)}, u32[]{:S(2)}, u32[]{:S(2)}) %collective-permute-start.4) | collective-permute-done | bytes 1679648 | tf_op jit(solution)/shard_map/ppermute | solution.py:49
  747.6 10.2 multiply_convert_fusion.2
  763.4 6.7 broadcast_select_fusion.11
  788.2 62.6 %all-reduce.32.cloned.1.call-done = (bf16[729,1152]{1,0:T(8,128)(2,1)}, bf16[729,1152]{1,0:T(8,128)(2,1)}) async-done(((bf16[729,1152]{1,0:T(8,128)(2,1)}, bf16[729,1152]{1,0:T(8,128)(2,1)}), (bf16[729,1152]{1,0:T(8,128)(2,1)}, bf16[729,1152]{1,0:T(8,128)(2,1)})) %all-reduce.32.cloned.1.call-update) | async-done | bytes 3359248 | tf_op jit(solution)/shard_map/psum | solution.py:254
  866.2 32.6 %collective-permute-done.3 = bf16[729,1152]{1,0:T(8,128)(2,1)S(1)} collective-permute-done((bf16[729,1152]{1,0:T(8,128)(2,1)S(1)}, bf16[729,1152]{1,0:T(8,128)(2,1)S(1)}, u32[]{:S(2)}, u32[]{:S(2)}) %collective-permute-start.3) | collective-permute-done | bytes 1679648 | tf_op jit(solution)/shard_map/ppermute | solution.py:49
  912.4 6.2 fusion.453
  922.9 33.5 %all-reduce.24.cloned.1.call-done = bf16[729,1152]{1,0:T(8,128)(2,1)} async-done(((bf16[729,1152]{1,0:T(8,128)(2,1)}), bf16[729,1152]{1,0:T(8,128)(2,1)}) %all-reduce.24.cloned.1.call-update) | async-done | bytes 1679632 | tf_op jit(solution)/shard_map/psum | solution.py:239
  967.1 6.6 convert_reduce_fusion.26
  978.5 10.2 multiply_convert_fusion.1
  1000.7 42.8 %all-reduce.26.cloned.1.call-done = bf16[729,1152]{1,0:T(8,128)(2,1)} async-done(((bf16[729,1152]{1,0:T(8,128)(2,1)}), bf16[729,1152]{1,0:T(8,128)(2,1)}) %all-reduce.26.cloned.1.call-update) | async-done | bytes 1679632 | tf_op jit(solution)/shard_map/psum | solution.py:254
  1056.3 34.5 %collective-permute-done.5 = bf16[729,1152]{1,0:T(8,128)(2,1)S(1)} collective-permute-done((bf16[729,1152]{1,0:T(8,128)(2,1)S(1)}, bf16[729,1152]{1,0:T(8,128)(2,1)S(1)}, u32[]{:S(2)}, u32[]{:S(2)}) %collective-permute-start.5) | collective-permute-done | bytes 1679648 | tf_op jit(solution)/shard_map/ppermute | solution.py:49
  1105.5 6.2 fusion.235
  1111.7 35.5 %all-reduce.28.cloned.1.call-done = bf16[729,1152]{1,0:T(8,128)(2,1)} async-done(((bf16[729,1152]{1,0:T(8,128)(2,1)}), bf16[729,1152]{1,0:T(8,128)(2,1)}) %all-reduce.28.cloned.1.call-update) | async-done | bytes 1679632 | tf_op jit(solution)/shard_map/psum | solution.py:239
  1167.0 10.2 multiply_convert_fusion
  1192.0 7.8 fusion.432
  1213.1 8.8 fusion.1
  1227.0 7.4 convolution_select_fusion.1
  1234.5 13.8 convolution_convert_fusion.4
  1248.2 7.8 fusion.295
  1264.8 8.6 fusion.5
  1275.3 34.3 %all_gather.10 = bf16[288,1152]{0,1:T(8,128)(2,1)S(1)} all-gather(bf16[288,288]{0,1:T(8,128)(2,1)} %bitcast.468), channel_id=1, replica_groups=mesh['pipe'=2,'dp'=4,'mp'=4] {'dp'}, dimensions={1}, use_global_device_ids=true | all-gather | bytes 829440 | tf_op jit(solution)/shard_map/all_gather | solution.py:370
  1314.0 15.9 reduce-scatter.9.cloned.1.call-done
  1329.9 75.1 %all-reduce.30.cloned.1.call-done = (bf16[729,1152]{1,0:T(8,128)(2,1)}, bf16[729,1152]{1,0:T(8,128)(2,1)}) async-done(((bf16[729,1152]{1,0:T(8,128)(2,1)}, bf16[729,1152]{1,0:T(8,128)(2,1)}), (bf16[729,1152]{1,0:T(8,128)(2,1)}, bf16[729,1152]{1,0:T(8,128)(2,1)})) %all-reduce.30.cloned.1.call-update) | async-done | bytes 3359248 | tf_op jit(solution)/shard_map/psum | solution.py:254
  1412.5 48.1 %reduce-scatter.11.cloned.1.call-done = bf16[1076,288]{0,1:T(8,128)(2,1)} async-done(((bf16[1076,1152]{0,1:T(8,128)(2,1)}), bf16[1076,288]{0,1:T(8,128)(2,1)}) %reduce-scatter.11.cloned.1.call-update) | async-done | bytes 619792 | tf_op jit(solution)/shard_map/reduce_scatter | solution.py:362
  1468.0 19.1 collective-permute-done.6
  1487.0 20.0 collective-permute-start.8
  1511.8 39.1 %all-reduce = (f32[1,1152]{1,0:T(1,128)}, f32[1,1152]{1,0:T(1,128)}, f32[1,2,288]{2,1,0:T(2,128)}, f32[1,1152]{1,0:T(1,128)}, f32[1,1152]{1,0:T(1,128)}, /*index...) all-reduce(f32[1,1152]{1,0:T(1,128)S(1)} %broadcast_in_dim.109, ...), channel_id=1, replica_groups=mesh['pipe'=2,'dp'=4,'mp'=4] {'dp'}, use_global_device_ids=true, to_apply=%region_80.81 | all-reduce | flops 8564 | bytes 68512 | tf_op jit(solution)/shard_map/psum | solution.py:378
  1558.3 60.4 %dynamic_update_slice.16 = bf16[1,1076,1152]{2,0,1:T(2,128)(2,1)} dynamic-update-slice(bf16[1,1076,1152]{2,0,1:T(2,128)(2,1)} %broadcast_in_dim.125, bf16[1,1076,288]{2,0,1:T(2,128)(2,1)} %copy.141, s32[]{:T(128)} %constant.138.clone.1, s32[]{:T(128)} %constant.138.clone.1, s32[]{:T(128)S(6)} %select_n.510) | dynamic-update-slice | bytes 1239556 | tf_op jit(solution)/shard_map/dynamic_update_slice | solution.py:20
  1628.1 189.2 %dynamic_update_slice.17 = bf16[1,1076,1152]{2,0,1:T(2,128)(2,1)} dynamic-update-slice(bf16[1,1076,1152]{2,0,1:T(2,128)(2,1)} %dynamic_update_slice.16, bf16[1,1076,288]{2,0,1:T(2,128)(2,1)} %copy.142, s32[]{:T(128)} %constant.138.clone.1, s32[]{:T(128)} %constant.138.clone.1, s32[]{:T(128)S(6)} %select_n.512) | dynamic-update-slice | bytes 1239556 | tf_op jit(solution)/shard_map/dynamic_update_slice | solution.py:28
  1817.3 189.8 %dynamic_update_slice.18 = bf16[1,1076,1152]{2,0,1:T(2,128)(2,1)} dynamic-update-slice(bf16[1,1076,1152]{2,0,1:T(2,128)(2,1)} %dynamic_update_slice.17, bf16[1,1076,288]{2,0,1:T(2,128)(2,1)} %copy.143, s32[]{:T(128)} %constant.138.clone.1, s32[]{:T(128)} %constant.138.clone.1, s32[]{:T(128)S(6)} %select_n.514) | dynamic-update-slice | bytes 1239556 | tf_op jit(solution)/shard_map/dynamic_update_slice | solution.py:37
  2011.8 189.8 %dynamic_update_slice.19 = bf16[1,1076,1152]{2,0,1:T(2,128)(2,1)} dynamic-update-slice(bf16[1,1076,1152]{2,0,1:T(2,128)(2,1)} %dynamic_update_slice.18, bf16[1,1076,288]{2,0,1:T(2,128)(2,1)} %copy.144, s32[]{:T(128)} %constant.138.clone.1, s32[]{:T(128)} %constant.138.clone.1, s32[]{:T(128)S(6)} %select_n.516) | dynamic-update-slice | bytes 1239556 | tf_op jit(solution)/shard_map/dynamic_update_slice | solution.py:28
  2201.5 7.2 broadcast_in_dim.131
  2220.9 12.7 copy.146
  (643 shorter events, 418.6 us)
Async XLA Ops:
  7.2 73.1 %copy-start = (bf16[1,1152,1076]{1,2,0:T(8,128)(2,1)S(1)}, bf16[1,1152,1076]{1,2,0:T(8,128)(2,1)}, u32[]{:S(2)}) copy-start(bf16[1,1152,1076]{1,2,0:T(8,128)(2,1)} %param.22) | copy-start | bytes 7437316
  7.2 67.8 %all-reduce.18.cloned.1.call-start = ((), (), s32[]{:S(2)}) async-start(), calls=%async_computation.4 | async-start | bytes 3391488 | tf_op jit(solution)/shard_map/psum | solution.py:182
  27.2 112.0 %all-reduce.20.cloned.1.call-start = ((), (), s32[]{:S(2)}) async-start(), calls=%async_computation.5 | async-start | bytes 3391488 | tf_op jit(solution)/shard_map/psum | solution.py:192
  94.0 154.4 %all-reduce.22.cloned.1.call-start = ((), (), s32[]{:S(2)}) async-start(), calls=%async_computation.6 | async-start | bytes 3391488 | tf_op jit(solution)/shard_map/psum | solution.py:182
  94.1 584.0 %copy-start.109 = (f32[1152]{0:T(1024)}, f32[1152]{0:T(1024)S(1)}, u32[]{:S(2)}) copy-start(f32[1152]{0:T(1024)S(1)} %convert_reduce_fusion.32) | copy-start | bytes 13828
  143.7 39.8 %collective-permute-start = (bf16[729,1152]{1,0:T(8,128)(2,1)}, bf16[729,1152]{1,0:T(8,128)(2,1)}, u32[]{:S(2)}, u32[]{:S(2)}) collective-permute-start(bf16[729,1152]{1,0:T(8,128)(2,1)} %add_convert_fusion.10), channel_id=1, source_target_pairs={{0,16},{1,17},{2,18},{3,19},{4,20},{5,21},{6,22},{7,23},{8,24},{9,... | collective-permute-start | bytes 5038856 | tf_op jit(solution)/shard_map/ppermute | solution.py:49
  201.8 155.2 %all-reduce.38.cloned.1.call-start = ((), (), s32[]{:S(2)}) async-start(), calls=%async_computation.20 | async-start | bytes 6782976 | tf_op jit(solution)/shard_map/psum | solution.py:239
  255.1 144.8 %copy-start.111 = (f32[729]{0:T(1024)}, f32[729]{0:T(1024)S(1)}, u32[]{:S(2)}) copy-start(f32[729]{0:T(1024)S(1)} %broadcast_multiply_fusion.28) | copy-start | bytes 8752
  255.6 144.3 %copy-start.117 = (f32[729]{0:T(1024)}, f32[729]{0:T(1024)S(1)}, u32[]{:S(2)}) copy-start(f32[729]{0:T(1024)S(1)} %add_rsqrt_fusion.12) | copy-start | bytes 8752
  284.1 234.9 %all-reduce.36.cloned.1.call-start = ((), (), s32[]{:S(2)}) async-start(), calls=%async_computation.19 | async-start | bytes 6782976 | tf_op jit(solution)/shard_map/psum | solution.py:254
  360.4 39.5 %collective-permute-start.2 = (bf16[729,1152]{1,0:T(8,128)(2,1)S(1)}, bf16[729,1152]{1,0:T(8,128)(2,1)S(1)}, u32[]{:S(2)}, u32[]{:S(2)}) collective-permute-start(bf16[729,1152]{1,0:T(8,128)(2,1)S(1)} %add_convert_fusion.7), channel_id=1, source_target_pairs={{0,16},{1,17},{2,18},{3,19},{4,20},{5,21},{6,22},{7,23},{8,24},{9,... | collective-permute-start | bytes 5038856 | tf_op jit(solution)/shard_map/ppermute | solution.py:49
  364.2 35.6 %slice-start = ((s8[5087232]{0:T(1024)(128)(4,1)}), s8[4194304]{0:T(1024)(128)(4,1)S(1)}, s32[]{:S(2)}) async-start(s8[5087232]{0:T(1024)(128)(4,1)} %bitcast.391), calls=%async_computation.21 | async-start | bytes 8388608
  364.2 35.6 %slice-start.1 = ((s8[5087232]{0:T(1024)(128)(4,1)}), s8[892928]{0:T(1024)(128)(4,1)S(1)}, s32[]{:S(2)}) async-start(s8[5087232]{0:T(1024)(128)(4,1)} %bitcast.391), calls=%async_computation.22 | async-start | bytes 1785856
  365.7 42.5 %copy-start.1 = (f32[4,729,729]{1,2,0:T(8,128)}, f32[4,729,729]{1,2,0:T(8,128)S(1)}, u32[]{:S(2)}) copy-start(f32[4,729,729]{1,2,0:T(8,128)S(1)} %fusion.450) | copy-start | bytes 25509172
  445.1 233.0 %all-reduce.34.cloned.1.call-start = ((), (), s32[]{:S(2)}) async-start(), calls=%async_computation.18 | async-start | bytes 6782976 | tf_op jit(solution)/shard_map/psum | solution.py:239
  445.2 81.9 %copy-start.115 = (f32[729]{0:T(1024)}, f32[729]{0:T(1024)S(1)}, u32[]{:S(2)}) copy-start(f32[729]{0:T(1024)S(1)} %broadcast_multiply_fusion.25) | copy-start | bytes 8752
  447.2 79.8 %copy-start.121 = (f32[729]{0:T(1024)}, f32[729]{0:T(1024)S(1)}, u32[]{:S(2)}) copy-start(f32[729]{0:T(1024)S(1)} %add_rsqrt_fusion.11) | copy-start | bytes 8752
  527.0 40.8 %collective-permute-start.1 = (bf16[729,1152]{1,0:T(8,128)(2,1)}, bf16[729,1152]{1,0:T(8,128)(2,1)}, u32[]{:S(2)}, u32[]{:S(2)}) collective-permute-start(bf16[729,1152]{1,0:T(8,128)(2,1)} %fusion.121), channel_id=1, source_target_pairs={{16,0},{17,1},{18,2},{19,3},{20,4},{21,5},{22,6},{23,7},{24,8},{25... | collective-permute-start | bytes 5038856 | tf_op jit(solution)/shard_map/ppermute | solution.py:49
  528.3 39.5 %copy-start.4 = (bf16[729,1152]{1,0:T(8,128)(2,1)S(1)}, bf16[729,1152]{1,0:T(8,128)(2,1)}, u32[]{:S(2)}) copy-start(bf16[729,1152]{1,0:T(8,128)(2,1)} %get-tuple-element.155) | copy-start | bytes 5038852
  528.4 39.5 %copy-start.41 = (bf16[729,1152]{1,0:T(8,128)(2,1)S(1)}, bf16[729,1152]{1,0:T(8,128)(2,1)}, u32[]{:S(2)}) copy-start(bf16[729,1152]{1,0:T(8,128)(2,1)} %all-reduce.18.cloned.1.call-done) | copy-start | bytes 5038852
  574.6 112.8 %copy-start.113 = (f32[729]{0:T(1024)}, f32[729]{0:T(1024)S(1)}, u32[]{:S(2)}) copy-start(f32[729]{0:T(1024)S(1)} %broadcast_multiply_fusion.20) | copy-start | bytes 8752
  576.8 110.6 %copy-start.119 = (f32[729]{0:T(1024)}, f32[729]{0:T(1024)S(1)}, u32[]{:S(2)}) copy-start(f32[729]{0:T(1024)S(1)} %add_rsqrt_fusion.8) | copy-start | bytes 8752
  606.1 244.8 %all-reduce.32.cloned.1.call-start = ((), (), s32[]{:S(2)}) async-start(), calls=%async_computation.17 | async-start | bytes 6782976 | tf_op jit(solution)/shard_map/psum | solution.py:254
  681.6 39.7 %collective-permute-start.4 = (bf16[729,1152]{1,0:T(8,128)(2,1)S(1)}, bf16[729,1152]{1,0:T(8,128)(2,1)S(1)}, u32[]{:S(2)}, u32[]{:S(2)}) collective-permute-start(bf16[729,1152]{1,0:T(8,128)(2,1)S(1)} %add_convert_fusion.4), channel_id=1, source_target_pairs={{0,16},{1,17},{2,18},{3,19},{4,20},{5,21},{6,22},{7,23},{8,24},{9,... | collective-permute-start | bytes 5038856 | tf_op jit(solution)/shard_map/ppermute | solution.py:49
  777.0 179.5 %all-reduce.24.cloned.1.call-start = ((), (), s32[]{:S(2)}) async-start(), calls=%async_computation.7 | async-start | bytes 3391488 | tf_op jit(solution)/shard_map/psum | solution.py:239
  858.2 40.6 %collective-permute-start.3 = (bf16[729,1152]{1,0:T(8,128)(2,1)S(1)}, bf16[729,1152]{1,0:T(8,128)(2,1)S(1)}, u32[]{:S(2)}, u32[]{:S(2)}) collective-permute-start(bf16[729,1152]{1,0:T(8,128)(2,1)S(1)} %fusion.114), channel_id=1, source_target_pairs={{16,0},{17,1},{18,2},{19,3},{20,4},{21,5},{22,6},{23,7},{24,8},{25... | collective-permute-start | bytes 5038856 | tf_op jit(solution)/shard_map/ppermute | solution.py:49
  866.2 40.8 %copy-start.173 = (f32[729,1076]{0,1:T(8,128)}, f32[729,1076]{0,1:T(8,128)S(1)}, u32[]{:S(2)}) copy-start(f32[729,1076]{0,1:T(8,128)S(1)} %convolution_add_fusion.3) | copy-start | bytes 9412852
  912.1 131.3 %all-reduce.26.cloned.1.call-start = ((), (), s32[]{:S(2)}) async-start(), calls=%async_computation.8 | async-start | bytes 3391488 | tf_op jit(solution)/shard_map/psum | solution.py:254
  998.4 148.8 %all-reduce.28.cloned.1.call-start = ((), (), s32[]{:S(2)}) async-start(), calls=%async_computation.9 | async-start | bytes 3391488 | tf_op jit(solution)/shard_map/psum | solution.py:239
  1050.2 40.7 %collective-permute-start.5 = (bf16[729,1152]{1,0:T(8,128)(2,1)S(1)}, bf16[729,1152]{1,0:T(8,128)(2,1)S(1)}, u32[]{:S(2)}, u32[]{:S(2)}) collective-permute-start(bf16[729,1152]{1,0:T(8,128)(2,1)S(1)} %fusion.107), channel_id=1, source_target_pairs={{16,0},{17,1},{18,2},{19,3},{20,4},{21,5},{22,6},{23,7},{24,8},{25... | collective-permute-start | bytes 5038856 | tf_op jit(solution)/shard_map/ppermute | solution.py:49
  1056.3 41.6 %copy-start.175 = (f32[729,1076]{0,1:T(8,128)}, f32[729,1076]{0,1:T(8,128)S(1)}, u32[]{:S(2)}) copy-start(f32[729,1076]{0,1:T(8,128)S(1)} %convolution_add_fusion.2) | copy-start | bytes 9412852
  1056.3 36.6 %copy-start.155 = (bf16[1,1076,1152]{2,1,0:T(8,128)(2,1)S(1)}, bf16[1,1076,1152]{2,1,0:T(8,128)(2,1)}, u32[]{:S(2)}) copy-start(bf16[1,1076,1152]{2,1,0:T(8,128)(2,1)} %param.24) | copy-start | bytes 7437316
  1103.0 170.7 %reduce-scatter.13.cloned.1.call-start = ((), (), s32[]{:S(2)}) async-start(), calls=%async_computation.14 | async-start | bytes 2580480 | tf_op jit(solution)/shard_map/reduce_scatter | solution.py:353
  1191.7 83.5 %reduce-scatter.15.cloned.1.call-start = ((), (), s32[]{:S(2)}) async-start(), calls=%async_computation.15 | async-start | bytes 1105920
  1213.0 116.9 %reduce-scatter.9.cloned.1.call-start = ((), (), s32[]{:S(2)}) async-start(), calls=%async_computation.11 | async-start | bytes 3317760 | tf_op jit(solution)/shard_map/reduce_scatter | solution.py:359
  1226.6 178.5 %all-reduce.30.cloned.1.call-start = ((), (), s32[]{:S(2)}) async-start(), calls=%async_computation.16 | async-start | bytes 6782976 | tf_op jit(solution)/shard_map/psum | solution.py:254
  1259.3 201.2 %reduce-scatter.11.cloned.1.call-start = ((), (), s32[]{:S(2)}) async-start(), calls=%async_computation.13 | async-start | bytes 3317760 | tf_op jit(solution)/shard_map/reduce_scatter | solution.py:362
  1273.6 935.2 %all-gather.3.cloned.1.call-start = ((), (), s32[]{:S(2)}) async-start(), calls=%async_computation.10 | async-start | bytes 2580480 | tf_op jit(solution)/shard_map/all_gather | solution.py:367
  1274.1 942.4 %all-gather.5.cloned.1.call-start = ((), (), s32[]{:S(2)}) async-start(), calls=%async_computation.12 | async-start | bytes 3317760 | tf_op jit(solution)/shard_map/all_gather | solution.py:373
  1408.8 52.3 %copy-start.110 = (f32[1152]{0:T(1024)S(1)}, f32[1152]{0:T(1024)}, u32[]{:S(2)}) copy-start(f32[1152]{0:T(1024)} %copy-done.109) | copy-start | bytes 13828
  1460.6 26.5 %collective-permute-start.6 = (bf16[1076,288]{0,1:T(8,128)(2,1)}, bf16[1076,288]{0,1:T(8,128)(2,1)}, u32[]{:S(2)}, u32[]{:S(2)}) collective-permute-start(bf16[1076,288]{0,1:T(8,128)(2,1)} %reduce-scatter.11.cloned.1.call-done), channel_id=1, source_target_pairs={{0,4},{4,8},{8,12},{12,0},{1,5},{5,9},{9,13},{13,1},{2,6},{6,10},{... | collective-permute-start | bytes 1859336 | tf_op jit(solution)/shard_map/ppermute | solution.py:25
  1461.1 45.9 %copy-start.55 = (bf16[729,1152]{1,0:T(8,128)(2,1)S(1)}, bf16[729,1152]{1,0:T(8,128)(2,1)}, u32[]{:S(2)}) copy-start(bf16[729,1152]{1,0:T(8,128)(2,1)} %copy-done.54) | copy-start | bytes 5038852
  1461.1 45.9 %copy-start.57 = (bf16[729,1152]{1,0:T(8,128)(2,1)S(1)}, bf16[729,1152]{1,0:T(8,128)(2,1)}, u32[]{:S(2)}) copy-start(bf16[729,1152]{1,0:T(8,128)(2,1)} %copy-done.56) | copy-start | bytes 5038852
  1461.1 45.9 %copy-start.59 = (bf16[729,1152]{1,0:T(8,128)(2,1)S(1)}, bf16[729,1152]{1,0:T(8,128)(2,1)}, u32[]{:S(2)}) copy-start(bf16[729,1152]{1,0:T(8,128)(2,1)} %copy-done.58) | copy-start | bytes 5038852
  1461.1 45.9 %copy-start.61 = (bf16[729,1152]{1,0:T(8,128)(2,1)S(1)}, bf16[729,1152]{1,0:T(8,128)(2,1)}, u32[]{:S(2)}) copy-start(bf16[729,1152]{1,0:T(8,128)(2,1)} %copy-done.60) | copy-start | bytes 5038852
  1464.6 154.1 %collective-permute-start.7 = (bf16[1076,288]{0,1:T(8,128)(2,1)}, bf16[1076,288]{0,1:T(8,128)(2,1)}, u32[]{:S(2)}, u32[]{:S(2)}) collective-permute-start(bf16[1076,288]{0,1:T(8,128)(2,1)} %reduce-scatter.11.cloned.1.call-done), channel_id=1, source_target_pairs={{0,12},{4,0},{8,4},{12,8},{1,13},{5,1},{9,5},{13,9},{2,14},{6,2},{... | collective-permute-start | bytes 1859336 | tf_op jit(solution)/shard_map/ppermute | solution.py:32
  1487.0 520.1 %collective-permute-start.8 = (bf16[1076,288]{0,1:T(8,128)(2,1)}, bf16[1076,288]{0,1:T(8,128)(2,1)}, u32[]{:S(2)}, u32[]{:S(2)}) collective-permute-start(bf16[1076,288]{0,1:T(8,128)(2,1)} %collective-permute-done.6), channel_id=1, source_target_pairs={{0,4},{4,8},{8,12},{12,0},{1,5},{5,9},{9,13},{13,1},{2,6},{6,10},{... | collective-permute-start | bytes 1859336 | tf_op jit(solution)/shard_map/ppermute | solution.py:25
  1507.1 43.8 %copy-start.103 = (bf16[1076,288]{0,1:T(8,128)(2,1)S(1)}, bf16[1076,288]{0,1:T(8,128)(2,1)}, u32[]{:S(2)}) copy-start(bf16[1076,288]{0,1:T(8,128)(2,1)} %reduce-scatter.11.cloned.1.call-done) | copy-start | bytes 1859332
  (165 other events, 748.6 us)
Sparse Core Ops, SparseCore 0:
  27.3 47.6 all-reduce.17
  94.1 44.9 all-reduce.19
  201.9 46.4 all-reduce.21
  284.2 72.6 all-reduce.37
  445.2 73.7 all-reduce.35
  606.2 71.8 all-reduce.33
  777.1 73.7 all-reduce.31
  912.2 44.1 all-reduce.23
  998.5 44.9 all-reduce.25
  1103.1 44.0 all-reduce.27
  1191.9 43.1 reduce-scatter.12
  1237.2 23.8 reduce-scatter.14
  1264.0 65.8 reduce-scatter.8
  1332.8 72.1 all-reduce.29
  1407.8 52.7 reduce-scatter.10
  1462.0 79.3 all-gather.2
  1542.9 53.4 all-gather.4
